TPU v7x, 32 devices: a whole 2x2x4 slice. The times are simulated.
32 devices in a mesh: cell: 4 (over z), spot: 8 (over y, x, core).
Axes of the slice: x: 2, y: 2, z: 4, core: 2. Of those that a mesh axis runs over, the one named last changes fastest.
Arguments:
- logits: float32 [4096, 4096], P('cell', 'spot'), may hold values from -4 to 330
- first_moment: bfloat16 [4096, 4096], P('cell', 'spot'), may hold values from -3 to 3
- second_moment: bfloat16 [4096, 4096], P('cell', 'spot'), may hold values from 0.049804688 to 1
- cell_expr: bfloat16 [4096, 128], P('cell'), may hold values from -36 to 36
- spot_expr: float32 [4096, 128], P('spot'), may hold values from -500 to 500
Outputs:
- new_logits: float32 [4096, 4096], P('cell', 'spot')
- new_first_moment: bfloat16 [4096, 4096], P('cell', 'spot')
- new_second_moment: bfloat16 [4096, 4096], P('cell', 'spot')
All inputs are finite; a program needn't handle non-finite values.
Results may differ from a plain program's by a relative error of at most 0.0052.
Values may be sent and summed in bfloat16 or wider, within the bound.
A program may use at most 64 MiB of HBM per device.

v0:
```python
import jax
import jax.numpy as jnp
from jax import lax
from jax.sharding import PartitionSpec as P

beta_one = 0.9
beta_two = 0.99
learn_rate = 0.1
adam_epsilon = 1e-08
norm_epsilon = 1e-06
adam_count = 10


def joined(value, axis, join):
    pieces = jax.tree.map(lambda part: lax.all_gather(part, axis), value)
    head = jax.tree.map(lambda part: part[0], pieces)
    tail = jax.tree.map(lambda part: part[1:], pieces)
    running, _ = lax.scan(lambda running, piece: (join(running, piece), None), head, tail)
    return running


def spot_term(predicted, target):
    spot_dot = jnp.sum(predicted * target, axis=1, keepdims=True)
    spot_pred = jnp.sum(predicted * predicted, axis=1, keepdims=True)
    spot_target = jnp.sum(target * target, axis=1, keepdims=True)
    return (target - spot_dot / (spot_pred + norm_epsilon) * predicted) / jnp.sqrt(
        (spot_pred + norm_epsilon) * (spot_target + norm_epsilon)
    )


def gene_partials(predicted, target):
    return (
        jnp.sum(predicted * target, axis=0),
        jnp.sum(predicted * predicted, axis=0),
        jnp.sum(target * target, axis=0),
    )


def gene_term(predicted, target, gene_dot, gene_pred, gene_target):
    gene_dot = gene_dot[None, :]
    gene_pred = gene_pred[None, :]
    gene_target = gene_target[None, :]
    return (target - gene_dot / (gene_pred + norm_epsilon) * predicted) / jnp.sqrt(
        (gene_pred + norm_epsilon) * (gene_target + norm_epsilon)
    )


def body(logits, first_moment, second_moment, cell_expr, spot_expr):
    cells = logits.shape[0] * lax.axis_size("cell")
    spots = logits.shape[1] * lax.axis_size("spot")
    genes = cell_expr.shape[1]
    loss_weight = jnp.sqrt(jnp.float32(genes * cells))
    ratio = spots / genes
    local_max = jnp.max(logits, axis=1)
    local_expo = jnp.exp(logits - local_max[:, None])
    local_total = jnp.sum(local_expo, axis=1)

    def combine(earlier, later):
        larger = jnp.maximum(earlier[0], later[0])
        return (
            larger,
            earlier[1] * jnp.exp(earlier[0] - larger) + later[1] * jnp.exp(later[0] - larger),
        )

    row_max, row_total = joined((local_max, local_total), "spot", combine)
    probs = local_expo * (jnp.exp(local_max - row_max) / row_total)[:, None]
    weights = probs.astype(jnp.bfloat16)
    partial_value = jnp.einsum("cs,cg->sg", weights, cell_expr, preferred_element_type=jnp.float32)
    predicted = lax.psum(partial_value, "cell")
    gene_dot, gene_pred, gene_target = lax.psum(gene_partials(predicted, spot_expr), "spot")
    pred_grad = -loss_weight * (
        spot_term(predicted, spot_expr)
        + ratio * gene_term(predicted, spot_expr, gene_dot, gene_pred, gene_target)
    )
    grad_rounded = pred_grad.astype(jnp.bfloat16)
    prob_grad = jnp.einsum("cg,sg->cs", cell_expr, grad_rounded, preferred_element_type=jnp.float32)
    row_dot = lax.psum(jnp.sum(probs * prob_grad, axis=1), "spot")
    logit_grad = probs * (prob_grad - row_dot[:, None])
    first_new = beta_one * first_moment.astype(jnp.float32) + (1.0 - beta_one) * logit_grad
    second_new = (
        beta_two * second_moment.astype(jnp.float32) + (1.0 - beta_two) * logit_grad * logit_grad
    )
    first_hat = first_new / (1.0 - beta_one**adam_count)
    second_hat = second_new / (1.0 - beta_two**adam_count)
    stepped = logits - learn_rate * first_hat / (jnp.sqrt(second_hat) + adam_epsilon)
    return (stepped, first_new.astype(jnp.bfloat16), second_new.astype(jnp.bfloat16))


def solution(mesh):
    placed = (
        P("cell", "spot"),
        P("cell", "spot"),
        P("cell", "spot"),
        P("cell", None),
        P("spot", None),
    )
    return jax.shard_map(
        body,
        mesh=mesh,
        in_specs=placed,
        out_specs=(P("cell", "spot"), P("cell", "spot"), P("cell", "spot")),
        check_vma=False,
    )
```

profile of v0, /device:TPU:0, one launch (start us, length us, event | category | flops | bytes accessed | tf_op | source)
XLA Modules:
  0.0 115.3 jit_solution(10364391293943496952)
XLA Ops:
  7.2 0.0 copy-start
  7.2 0.0 all-reduce.3.cloned.1.call-start
  7.2 2.0 %copy.18 = f32[1024,512]{0,1:T(8,128)S(1)} copy(f32[1024,512]{1,0:T(8,128)} %param.7) | data formatting | bytes 4194304 | tf_op args[0]
  9.2 1.8 %reduce_max.9 = f32[1024]{0:T(1024)S(1)} reduce(f32[1024,512]{1,0:T(8,128)} %param.7, f32[]{:T(128)} %constant.8.clone.1), dimensions={1}, to_apply=%region_0.0 | reduce | flops 523264 | bytes 2101252 | tf_op jit(solution)/shard_map/reduce_max | solution.py:54
  11.0 0.3 fusion.4
  11.3 10.6 %all-gather.1 = f32[8192]{0:T(1024)S(1)} all-gather(f32[1024]{0:T(1024)S(1)} %fusion.4), channel_id=3, replica_groups=mesh['cell'=4,'spot'=8] {'spot'}, dimensions={0}, use_global_device_ids=true | all-gather | bytes 36864 | tf_op jit(solution)/shard_map/all_gather | solution.py:15
  21.9 9.1 %all-gather = f32[8192]{0:T(1024)S(1)} all-gather(f32[1024]{0:T(1024)S(1)} %reduce_max.9), channel_id=2, replica_groups=mesh['cell'=4,'spot'=8] {'spot'}, dimensions={0}, use_global_device_ids=true | all-gather | bytes 36864 | tf_op jit(solution)/shard_map/all_gather | solution.py:15
  31.0 0.4 while.12
  31.4 0.0 copy-done
  31.4 1.2 %fusion.8 = f32[512,128]{1,0:T(8,128)} fusion(bf16[1024,128]{1,0:T(8,128)(2,1)S(1)} %copy-done, f32[1024,512]{0,1:T(8,128)S(1)} %copy.18, f32[1024]{0:T(1024)S(1)} %exponential_divide_fusion, f32[1024]{0:T(1024)S(1)} %reduce_max.9), kind=kOutput, calls=%fused_computation.17 | convolution fusion | flops 135790592 | bytes 2629632 | tf_op jit(solution)/shard_map/cs,cg->sg/dot_general | solution.py:68
  32.6 0.0 all-reduce.3.cloned.1.call-update
  32.6 1.5 %copy.15 = bf16[1024,512]{0,1:T(8,128)(2,1)S(1)} copy(bf16[1024,512]{1,0:T(8,128)(2,1)} %param.8) | data formatting | bytes 2097152 | tf_op args[1]
  34.1 2.3 %copy.17 = bf16[1024,512]{0,1:T(8,128)(2,1)} copy(bf16[1024,512]{1,0:T(8,128)(2,1)} %param.9) | data formatting | bytes 2097152 | tf_op args[2]
  36.4 32.3 %all-reduce.3.cloned.1.call-done = f32[512,128]{1,0:T(8,128)} async-done(((f32[512,128]{1,0:T(8,128)}), f32[512,128]{1,0:T(8,128)}) %all-reduce.3.cloned.1.call-update) | async-done | bytes 262160 | tf_op jit(solution)/shard_map/psum | solution.py:69
  68.6 1.3 %multiply_reduce_fusion.5 = (f32[512]{0:T(512)S(1)}, f32[128]{0:T(128)S(1)}, f32[128]{0:T(128)S(1)}, f32[512]{0:T(512)S(1)}, f32[128]{0:T(128)S(1)}, /*index=5*/f32[512]{0:T(512)S(1)}) fusion(f32[512,128]{1,0:T(8,128)} %all-reduce.3.cloned.1.call-done, f32[512,128]{1,0:T(8,128)} %param.11), kind=kLoop, calls=%fused_computation.33 | loop fusion | flops 587904 | bytes 531968 | tf_op jit(solution)/shard_map/reduce_sum | solution.py:23
  70.0 11.8 %all-reduce = (f32[128]{0:T(128)S(1)}, f32[128]{0:T(128)S(1)}, f32[128]{0:T(128)S(1)}) all-reduce(f32[128]{0:T(128)S(1)} %get-tuple-element.41, f32[128]{0:T(128)S(1)} %get-tuple-element.43, f32[128]{0:T(128)S(1)} %get-tuple-element.40), channel_id=1, replica_groups=mesh['cell'=4,'spot'=8] {'spot'}, use_global_device_ids=true, to_apply=%region_13.14 | all-reduce | flops 384 | bytes 3072 | tf_op jit(solution)/shard_map/psum | solution.py:70
  81.8 2.9 %fusion.1 = (f32[1024]{0:T(1024)S(1)}, f32[512,1024]{1,0:T(8,128)}) fusion(f32[1024,512]{0,1:T(8,128)S(1)} %copy.18, f32[1024]{0:T(1024)S(1)} %exponential_divide_fusion, f32[1024]{0:T(1024)S(1)} %reduce_max.9, bf16[1024,128]{1,0:T(8,128)(2,1)S(1)} %copy-done, f32[512,128]{1,0:T(8,128)} %param.11, f32[512,128]{1,0:T(8,128)} %all-reduce.3.cloned.1.call-done, ...), kind=kOutput, calls=%fused_computation.7 | convolution fusion | flops 136969216 | bytes 4998144 | tf_op jit(solution)/shard_map/cg,sg->cs/dot_general | solution.py:76
  84.7 11.8 %psum.39 = f32[1024]{0:T(1024)S(1)} all-reduce(f32[1024]{0:T(1024)S(1)} %get-tuple-element.69), channel_id=1, replica_groups=mesh['cell'=4,'spot'=8] {'spot'}, use_global_device_ids=true, to_apply=%region_15.16 | all-reduce | flops 1024 | bytes 8192 | tf_op jit(solution)/shard_map/psum | solution.py:77
  96.5 6.3 %fusion.7 = (bf16[1024,512]{0,1:T(8,128)(2,1)}, f32[1024,512]{0,1:T(8,128)}, bf16[1024,512]{0,1:T(8,128)(2,1)}) fusion(bf16[1024,512]{0,1:T(8,128)(2,1)} %copy.17, f32[1024]{0:T(1024)S(1)} %psum.39, f32[512,1024]{1,0:T(8,128)} %get-tuple-element.70, f32[1024]{0:T(1024)S(1)} %exponential_divide_fusion, f32[1024,512]{0,1:T(8,128)S(1)} %copy.18, ...), kind=kLoop, calls=%fused_computation.16 | loop fusion | flops 10485760 | bytes 10498048 | tf_op jit(solution)/shard_map/convert_element_type | solution.py:86
  102.9 3.0 %copy.19 = f32[1024,512]{1,0:T(8,128)} copy(f32[1024,512]{0,1:T(8,128)} %get-tuple-element.63) | data formatting | bytes 4194304
  105.8 0.0 copy-done.2
  105.9 1.3 %copy.20 = bf16[1024,512]{1,0:T(8,128)(2,1)} copy(bf16[1024,512]{0,1:T(8,128)(2,1)S(1)} %copy-done.2) | data formatting | bytes 2097152
  107.2 0.0 copy-done.1
  107.2 1.3 %copy.21 = bf16[1024,512]{1,0:T(8,128)(2,1)} copy(bf16[1024,512]{0,1:T(8,128)(2,1)S(1)} %copy-done.1) | data formatting | bytes 2097152
  (25 shorter events, 0.2 us)
Async XLA Ops:
  7.2 24.2 %copy-start = (bf16[1024,128]{1,0:T(8,128)(2,1)S(1)}, bf16[1024,128]{1,0:T(8,128)(2,1)}, u32[]{:S(2)}) copy-start(bf16[1024,128]{1,0:T(8,128)(2,1)} %param.10) | copy-start | bytes 786436
  7.2 61.5 %all-reduce.3.cloned.1.call-start = ((), (), s32[]{:S(2)}) async-start(), calls=%async_computation | async-start | bytes 524288 | tf_op jit(solution)/shard_map/psum | solution.py:69
  102.9 3.0 %copy-start.2 = (bf16[1024,512]{0,1:T(8,128)(2,1)S(1)}, bf16[1024,512]{0,1:T(8,128)(2,1)}, u32[]{:S(2)}) copy-start(bf16[1024,512]{0,1:T(8,128)(2,1)} %get-tuple-element.64) | copy-start | bytes 3145732
  105.8 1.3 %copy-start.1 = (bf16[1024,512]{0,1:T(8,128)(2,1)S(1)}, bf16[1024,512]{0,1:T(8,128)(2,1)}, u32[]{:S(2)}) copy-start(bf16[1024,512]{0,1:T(8,128)(2,1)} %get-tuple-element.62) | copy-start | bytes 3145732
Sparse Core Ops, SparseCore 0:
  32.7 35.8 all-reduce.2
where the time goes:
time: 116 us; the launch traced here: 115 us
  blocking collectives  43.3 us (37%)
  waiting for transfers between devices  32.3 us (28%)
  between operations  14.1 us (12%)
  local copies, waits for them, and re-layouts  11.4 us (10%)
  other arithmetic  9.89 us (9%)
  matrix products  4.08 us (4%)
    psum x1, waiting for transfers between devices, body(): predicted = lax.psum(partial_value, 'cell')  32.3 us
    all_gather x2, blocking collectives, joined(): pieces = jax.tree.map(lambda part: lax.all_gather(part, axis), value)  19.7 us
    psum x1, blocking collectives, body(): lax.psum(gene_partials(predicted, spot_expr), 'spot')  11.8 us
    psum x1, blocking collectives, body(): row_dot = lax.psum(jnp.sum(probs * prob_grad, axis=1), 'spot')  11.8 us
    unnamed x12, local copies, waits for them, and re-layouts  11.3 us
    convert_element_type x1, other arithmetic, body(): second_new.astype(jnp.bfloat16)  6.33 us
    dot_general x1, matrix products, body(): jnp.einsum('cg,sg->cs', cell_expr, grad_rounded, preferred_element_type=j...  2.89 us
  transfers between devices with their start and end apart: 1, of which 1 were waited for; matrix products, arithmetic and copies ran while one was open for 3% of the time, Pallas kernels for 0%

commit v1 on v0

--- a/solution.py
+++ b/solution.py
@@ -66,7 +66,11 @@
     probs = local_expo * (jnp.exp(local_max - row_max) / row_total)[:, None]
     weights = probs.astype(jnp.bfloat16)
     partial_value = jnp.einsum("cs,cg->sg", weights, cell_expr, preferred_element_type=jnp.float32)
-    predicted = lax.psum(partial_value, "cell")
+    predicted = partial_value
+    for hop in (1, 2):
+        predicted = predicted + lax.ppermute(
+            predicted, "cell", [(dev, dev ^ hop) for dev in range(4)]
+        )
     gene_dot, gene_pred, gene_target = lax.psum(gene_partials(predicted, spot_expr), "spot")
     pred_grad = -loss_weight * (
         spot_term(predicted, spot_expr)

time: 116 us -> 89.9 us (0.78)
  waiting for transfers between devices: 32.3 us -> 15.2 us
  between operations: 14.1 us -> 0.71 us
  starting transfers between devices: 0.04 us -> 4.23 us
  other arithmetic: 9.89 us -> 11.2 us
    psum x1 -> x0, waiting for transfers between devices: 32.3 us -> none  [body(): predicted = lax.psum(partial_value, 'cell')]
    ppermute x0 -> x2, waiting for transfers between devices: none -> 15.2 us  [body(): lax.ppermute(predicted, 'cell', [(dev, dev ^ hop) for dev in range(4)])]
    ppermute x0 -> x2, starting transfers between devices: none -> 4.23 us  [body(): lax.ppermute(predicted, 'cell', [(dev, dev ^ hop) for dev in range(4)])]
  transfers between devices with their start and end apart: 1 -> 2, of which waited for: 1 -> 2; matrix products, arithmetic and copies ran while one was open for 3% -> 4% of each run, Pallas kernels for 0% -> 0%
where the time goes in v1:
time: 89.9 us; the launch traced here: 89.6 us
  blocking collectives  43.3 us (48%)
  waiting for transfers between devices  15.2 us (17%)
  local copies, waits for them, and re-layouts  11.4 us (13%)
  other arithmetic  11.2 us (12%)
  starting transfers between devices  4.23 us (5%)
  matrix products  3.36 us (4%)
    all_gather x2, blocking collectives, joined(): pieces = jax.tree.map(lambda part: lax.all_gather(part, axis), value)  19.7 us
    ppermute x2, waiting for transfers between devices, body(): lax.ppermute(predicted, 'cell', [(dev, dev ^ hop) for dev in range(4)])  15.2 us
    psum x1, blocking collectives, body(): lax.psum(gene_partials(predicted, spot_expr), 'spot')  11.9 us
    psum x1, blocking collectives, body(): row_dot = lax.psum(jnp.sum(probs * prob_grad, axis=1), 'spot')  11.8 us
    unnamed x12, local copies, waits for them, and re-layouts  11.3 us
    convert_element_type x1, other arithmetic, body(): second_new.astype(jnp.bfloat16)  6.33 us
    ppermute x2, starting transfers between devices, body(): lax.ppermute(predicted, 'cell', [(dev, dev ^ hop) for dev in range(4)])  4.23 us
    dot_general x1, matrix products, body(): jnp.einsum('cg,sg->cs', cell_expr, grad_rounded, preferred_element_type=j...  2.89 us
  transfers between devices with their start and end apart: 2, of which 2 were waited for; matrix products, arithmetic and copies ran while one was open for 4% of the time, Pallas kernels for 0%

profile of v1, /device:TPU:0, one launch (start us, length us, event | category | flops | bytes accessed | tf_op | source)
XLA Modules:
  0.0 89.6 jit_solution(747260609627093647)
XLA Ops:
  0.6 0.0 copy-start
  0.6 2.0 %copy.18 = f32[1024,512]{0,1:T(8,128)S(1)} copy(f32[1024,512]{1,0:T(8,128)} %param.7) | data formatting | bytes 4194304 | tf_op args[0]
  2.6 1.8 %reduce_max.9 = f32[1024]{0:T(1024)S(1)} reduce(f32[1024,512]{1,0:T(8,128)} %param.7, f32[]{:T(128)} %constant.8.clone.1), dimensions={1}, to_apply=%region_0.0 | reduce | flops 523264 | bytes 2101252 | tf_op jit(solution)/shard_map/reduce_max | solution.py:54
  4.4 0.3 fusion.4
  4.8 10.6 %all-gather.1 = f32[8192]{0:T(1024)S(1)} all-gather(f32[1024]{0:T(1024)S(1)} %fusion.4), channel_id=3, replica_groups=mesh['cell'=4,'spot'=8] {'spot'}, dimensions={0}, use_global_device_ids=true | all-gather | bytes 36864 | tf_op jit(solution)/shard_map/all_gather | solution.py:15
  15.4 9.1 %all-gather = f32[8192]{0:T(1024)S(1)} all-gather(f32[1024]{0:T(1024)S(1)} %reduce_max.9), channel_id=2, replica_groups=mesh['cell'=4,'spot'=8] {'spot'}, dimensions={0}, use_global_device_ids=true | all-gather | bytes 36864 | tf_op jit(solution)/shard_map/all_gather | solution.py:15
  24.5 0.4 while.12
  24.8 0.0 copy-done
  24.9 0.5 fusion.8
  25.3 1.6 %collective-permute-start = (f32[512,128]{1,0:T(8,128)S(1)}, f32[512,128]{1,0:T(8,128)S(1)}, u32[]{:S(2)}, u32[]{:S(2)}) collective-permute-start(f32[512,128]{1,0:T(8,128)S(1)} %fusion.8), channel_id=1, source_target_pairs={{0,8},{8,0},{16,24},{24,16},{1,9},{9,1},{17,25},{25,17},{2,10},{10... | collective-permute-start | bytes 786440 | tf_op jit(solution)/shard_map/ppermute | solution.py:71
  27.0 7.0 %collective-permute-done = f32[512,128]{1,0:T(8,128)S(1)} collective-permute-done((f32[512,128]{1,0:T(8,128)S(1)}, f32[512,128]{1,0:T(8,128)S(1)}, u32[]{:S(2)}, u32[]{:S(2)}) %collective-permute-start) | collective-permute-done | bytes 262176 | tf_op jit(solution)/shard_map/ppermute | solution.py:71
  34.0 0.7 add.64
  34.7 2.6 %collective-permute-start.1 = (f32[512,128]{1,0:T(8,128)}, f32[512,128]{1,0:T(8,128)}, u32[]{:S(2)}, u32[]{:S(2)}) collective-permute-start(f32[512,128]{1,0:T(8,128)} %add.64), channel_id=1, source_target_pairs={{0,16},{8,24},{16,0},{24,8},{1,17},{9,25},{17,1},{25,9},{2,18},{10... | collective-permute-start | bytes 786440 | tf_op jit(solution)/shard_map/ppermute | solution.py:71
  37.3 1.5 %copy.15 = bf16[1024,512]{0,1:T(8,128)(2,1)S(1)} copy(bf16[1024,512]{1,0:T(8,128)(2,1)} %param.8) | data formatting | bytes 2097152 | tf_op args[1]
  38.8 2.3 %copy.17 = bf16[1024,512]{0,1:T(8,128)(2,1)} copy(bf16[1024,512]{1,0:T(8,128)(2,1)} %param.9) | data formatting | bytes 2097152 | tf_op args[2]
  41.0 8.2 %collective-permute-done.1 = f32[512,128]{1,0:T(8,128)} collective-permute-done((f32[512,128]{1,0:T(8,128)}, f32[512,128]{1,0:T(8,128)}, u32[]{:S(2)}, u32[]{:S(2)}) %collective-permute-start.1) | collective-permute-done | bytes 262176 | tf_op jit(solution)/shard_map/ppermute | solution.py:71
  49.2 1.9 %multiply_reduce_fusion.5 = (f32[512]{0:T(512)S(1)}, f32[128]{0:T(128)S(1)}, f32[128]{0:T(128)S(1)}, f32[512]{0:T(512)S(1)}, f32[128]{0:T(128)S(1)}, /*index=5*/f32[512]{0:T(512)S(1)}, f32[512,128]{1,0:T(8,128)}) fusion(f32[512,128]{1,0:T(8,128)} %param.11, f32[512,128]{1,0:T(8,128)} %add.64, f32[512,128]{1,0:T(8,128)} %collective-permute-done.1), kind=kLoop, calls=%fused_computation.33 | loop fusion | flops 653440 | bytes 1056256 | tf_op jit(solution)/shard_map/reduce_sum | solution.py:23
  51.1 11.9 %all-reduce = (f32[128]{0:T(128)S(1)}, f32[128]{0:T(128)S(1)}, f32[128]{0:T(128)S(1)}) all-reduce(f32[128]{0:T(128)S(1)} %get-tuple-element.41, f32[128]{0:T(128)S(1)} %get-tuple-element.43, f32[128]{0:T(128)S(1)} %get-tuple-element.40), channel_id=1, replica_groups=mesh['cell'=4,'spot'=8] {'spot'}, use_global_device_ids=true, to_apply=%region_12.13 | all-reduce | flops 384 | bytes 3072 | tf_op jit(solution)/shard_map/psum | solution.py:74
  63.0 2.9 %fusion.1 = (f32[1024]{0:T(1024)S(1)}, f32[512,1024]{1,0:T(8,128)}) fusion(f32[1024,512]{0,1:T(8,128)S(1)} %copy.18, f32[1024]{0:T(1024)S(1)} %exponential_divide_fusion, f32[1024]{0:T(1024)S(1)} %reduce_max.9, bf16[1024,128]{1,0:T(8,128)(2,1)S(1)} %copy-done, f32[512,128]{1,0:T(8,128)} %param.11, f32[512,128]{1,0:T(8,128)} %get-tuple-element.60, ...), kind=kOutput, calls=%fused_computation.7 | convolution fusion | flops 136969216 | bytes 4998144 | tf_op jit(solution)/shard_map/cg,sg->cs/dot_general | solution.py:80
  65.9 11.8 %psum.31 = f32[1024]{0:T(1024)S(1)} all-reduce(f32[1024]{0:T(1024)S(1)} %get-tuple-element.70), channel_id=1, replica_groups=mesh['cell'=4,'spot'=8] {'spot'}, use_global_device_ids=true, to_apply=%region_14.15 | all-reduce | flops 1024 | bytes 8192 | tf_op jit(solution)/shard_map/psum | solution.py:81
  77.6 6.3 %fusion.7 = (bf16[1024,512]{0,1:T(8,128)(2,1)}, f32[1024,512]{0,1:T(8,128)}, bf16[1024,512]{0,1:T(8,128)(2,1)}) fusion(bf16[1024,512]{0,1:T(8,128)(2,1)} %copy.17, f32[1024]{0:T(1024)S(1)} %psum.31, f32[512,1024]{1,0:T(8,128)} %get-tuple-element.71, f32[1024]{0:T(1024)S(1)} %exponential_divide_fusion, f32[1024,512]{0,1:T(8,128)S(1)} %copy.18, ...), kind=kLoop, calls=%fused_computation.16 | loop fusion | flops 10485760 | bytes 10498048 | tf_op jit(solution)/shard_map/convert_element_type | solution.py:90
  84.0 3.0 %copy.19 = f32[1024,512]{1,0:T(8,128)} copy(f32[1024,512]{0,1:T(8,128)} %get-tuple-element.64) | data formatting | bytes 4194304
  87.0 1.3 %copy.20 = bf16[1024,512]{1,0:T(8,128)(2,1)} copy(bf16[1024,512]{0,1:T(8,128)(2,1)S(1)} %copy-done.2) | data formatting | bytes 2097152
  88.3 1.3 %copy.21 = bf16[1024,512]{1,0:T(8,128)(2,1)} copy(bf16[1024,512]{0,1:T(8,128)(2,1)S(1)} %copy-done.1) | data formatting | bytes 2097152
  (27 shorter events, 0.2 us)
Async XLA Ops:
  0.6 24.2 %copy-start = (bf16[1024,128]{1,0:T(8,128)(2,1)S(1)}, bf16[1024,128]{1,0:T(8,128)(2,1)}, u32[]{:S(2)}) copy-start(bf16[1024,128]{1,0:T(8,128)(2,1)} %param.10) | copy-start | bytes 786436
  25.3 8.6 %collective-permute-start = (f32[512,128]{1,0:T(8,128)S(1)}, f32[512,128]{1,0:T(8,128)S(1)}, u32[]{:S(2)}, u32[]{:S(2)}) collective-permute-start(f32[512,128]{1,0:T(8,128)S(1)} %fusion.8), channel_id=1, source_target_pairs={{0,8},{8,0},{16,24},{24,16},{1,9},{9,1},{17,25},{25,17},{2,10},{10... | collective-permute-start | bytes 786440 | tf_op jit(solution)/shard_map/ppermute | solution.py:71
  34.7 14.5 %collective-permute-start.1 = (f32[512,128]{1,0:T(8,128)}, f32[512,128]{1,0:T(8,128)}, u32[]{:S(2)}, u32[]{:S(2)}) collective-permute-start(f32[512,128]{1,0:T(8,128)} %add.64), channel_id=1, source_target_pairs={{0,16},{8,24},{16,0},{24,8},{1,17},{9,25},{17,1},{25,9},{2,18},{10... | collective-permute-start | bytes 786440 | tf_op jit(solution)/shard_map/ppermute | solution.py:71
  84.0 3.0 %copy-start.2 = (bf16[1024,512]{0,1:T(8,128)(2,1)S(1)}, bf16[1024,512]{0,1:T(8,128)(2,1)}, u32[]{:S(2)}) copy-start(bf16[1024,512]{0,1:T(8,128)(2,1)} %get-tuple-element.65) | copy-start | bytes 3145732
  87.0 1.3 %copy-start.1 = (bf16[1024,512]{0,1:T(8,128)(2,1)S(1)}, bf16[1024,512]{0,1:T(8,128)(2,1)}, u32[]{:S(2)}) copy-start(bf16[1024,512]{0,1:T(8,128)(2,1)} %get-tuple-element.63) | copy-start | bytes 3145732
